TPU v7x, 32 devices: a whole 2x2x4 slice. The times are simulated.
32 devices in a mesh: tm: 16 (over z, x, core), rows: 2 (over y).
Axes of the slice: x: 2, y: 2, z: 4, core: 2. Of those that a mesh axis runs over, the one named last changes fastest.
Arguments:
- video: bfloat16 [32, 16, 480, 128], P('tm', 'rows'), may hold values from -1000 to 1000, as said below
- spatial_weight: bfloat16 [3, 3, 128, 128], replicated, may hold values from -0.1875 to 0.1875
- norm_gain: float32 [128], replicated, may hold values from 0.5 to 1.5
- norm_shift: float32 [128], replicated, may hold values from -3 to 3
- temporal_weight: bfloat16 [3, 3, 128, 128], replicated, may hold values from -0.3125 to 0.3125
Outputs:
- encoded: bfloat16 [32, 16, 480, 128], P('tm', 'rows')
Inputs may be any that keep to these rules, and one draw needn't show every extreme that they name: `video`: feature values are finite and of moderate size.
All inputs are finite; a program needn't handle non-finite values.
Results may differ from a plain program's by a relative error of at most 0.0065.
Values may be sent and summed in bfloat16 or wider, within the bound.
No kernel may reach another device: no remote copies, remote signals or barrier semaphores. Data moves between devices by JAX's collectives and lax.ppermute only.
A program may use at most 64 MiB of HBM per device.

v0:
```python
import jax
import jax.numpy as jnp
from jax import lax
from jax.sharding import PartitionSpec as P

GROUPS = 32


def padded_2(array, sides, width):
    for axis, dim in sides:
        size, length = (lax.axis_size(axis), array.shape[dim])
        up = [(i, (i + 1) % size) for i in range(size - 1)]
        down = [(j, i) for i, j in up]
        last = lax.slice_in_dim(array, length - width, length, axis=dim)
        leading = lax.slice_in_dim(array, 0, width, axis=dim)
        before = lax.ppermute(last, axis, up)
        after = lax.ppermute(leading, axis, down)
        array = jnp.concatenate([before, array, after], axis=dim)
    return array


def temporal_layer(extended, lead, dilation, kernels):
    own = extended.shape[0] - lead
    total = extended[lead:].astype(jnp.float32)
    for tap_index in range(3):
        start = lead - tap_index * dilation
        total = total + jnp.einsum(
            "trwc,cd->trwd",
            extended[start : start + own],
            kernels[tap_index],
            preferred_element_type=jnp.float32,
        )
    return total.astype(jnp.bfloat16)


def body(video, spatial_weight, norm_gain, norm_shift, temporal_weight):
    fr_local, band, width, chans = video.shape
    padded = padded_2(video, (("rows", 1),), 1)
    padded = jnp.pad(padded, ((0, 0), (0, 0), (1, 1), (0, 0)))
    pieces = [
        padded[:, row_tap : row_tap + band, col_tap : col_tap + width, :]
        for row_tap in range(3)
        for col_tap in range(3)
    ]
    patches = jnp.concatenate(pieces, axis=-1).reshape(fr_local * band * width, 9 * chans)
    conv = jnp.dot(
        patches, spatial_weight.reshape(9 * chans, chans), preferred_element_type=jnp.float32
    )
    per_group = chans // GROUPS
    grouped = conv.reshape(fr_local, band, width, GROUPS, per_group)
    part_sum = jnp.sum(grouped, axis=(1, 2, 4))
    part_square = jnp.sum(grouped * grouped, axis=(1, 2, 4))
    total_sum, total_square = lax.psum((part_sum, part_square), "rows")
    count = jnp.float32(band * lax.axis_size("rows") * width * per_group)
    mean = total_sum / count
    var = total_square / count - mean * mean
    normed = (grouped - mean[:, None, None, :, None]) * lax.rsqrt(var + 1e-05)[
        :, None, None, :, None
    ]
    normed = normed.reshape(fr_local, band, width, chans) * norm_gain + norm_shift
    hidden = jax.nn.silu(normed).astype(jnp.bfloat16)
    current = lax.all_to_all(hidden, "tm", split_axis=2, concat_axis=0, tiled=True)
    for layer, dilation in enumerate((1, 2, 4)):
        lead = 2 * dilation
        extended = jnp.pad(current, ((lead, 0), (0, 0), (0, 0), (0, 0)))
        current = temporal_layer(extended, lead, dilation, temporal_weight[layer])
    return lax.all_to_all(current, "tm", split_axis=0, concat_axis=2, tiled=True)


def solution(mesh):
    return jax.shard_map(
        body,
        mesh=mesh,
        in_specs=(P("tm", "rows", None, None), P(), P(), P(), P()),
        out_specs=P("tm", "rows", None, None),
        check_vma=False,
    )
```

profile of v0, /device:TPU:1, one launch (start us, length us, event | category | flops | bytes accessed | tf_op | source)
XLA Modules:
  0.0 154.6 jit_solution(4578269416225532073)
XLA Ops:
  0.0 1.1 fusion.36
  1.1 4.0 %collective-permute-start = (bf16[2,1,480,128]{3,2,1,0:T(8,128)(2,1)S(1)}, bf16[2,1,480,128]{3,2,1,0:T(8,128)(2,1)S(1)}, u32[]{:S(2)}, u32[]{:S(2)}) collective-permute-start(bf16[2,1,480,128]{3,2,1,0:T(8,128)(2,1)S(1)} %get-tuple-element.9), channel_id=1, source_target_pairs={{0,1},{2,3},{4,5},{6,7},{8,9},{10,11},{12,13},{14,15},{16,17},{18,... | collective-permute-start | bytes 737288 | tf_op jit(solution)/shard_map/ppermute | solution.py:16
  5.1 1.3 collective-permute-start.1
  6.4 1.2 copy.14
  7.6 0.1 dot_general.35
  7.6 0.0 copy-start
  7.7 2.0 %collective-permute-done = bf16[2,1,480,128]{3,2,1,0:T(8,128)(2,1)S(1)} collective-permute-done((bf16[2,1,480,128]{3,2,1,0:T(8,128)(2,1)S(1)}, bf16[2,1,480,128]{3,2,1,0:T(8,128)(2,1)S(1)}, u32[]{:S(2)}, u32[]{:S(2)}) %collective-permute-start) | collective-permute-done | bytes 245792 | tf_op jit(solution)/shard_map/ppermute | solution.py:16
  9.7 3.8 %collective-permute-done.1 = bf16[2,1,480,128]{3,2,1,0:T(8,128)(2,1)S(1)} collective-permute-done((bf16[2,1,480,128]{3,2,1,0:T(8,128)(2,1)S(1)}, bf16[2,1,480,128]{3,2,1,0:T(8,128)(2,1)S(1)}, u32[]{:S(2)}, u32[]{:S(2)}) %collective-permute-start.1) | collective-permute-done | bytes 245792 | tf_op jit(solution)/shard_map/ppermute | solution.py:17
  13.5 2.1 %fusion.7 = bf16[2,10,482,128]{3,2,1,0:T(8,128)(2,1)S(1)} fusion(bf16[2,1,480,128]{3,2,1,0:T(8,128)(2,1)S(1)} %collective-permute-done.1, bf16[2,8,480,128]{3,2,1,0:T(8,128)(2,1)} %param.5, bf16[2,1,480,128]{3,2,1,0:T(8,128)(2,1)S(1)} %collective-permute-done), kind=kLoop, calls=%fused_computation.15 | loop fusion | flops 14807040 | bytes 4925440 | tf_op jit(solution)/shard_map/concatenate | solution.py:18
  15.6 0.3 slice_dynamic-update-slice_fusion.5
  15.9 0.0 copy-done
  15.9 0.5 fusion.9
  16.4 0.8 slice_dynamic-update-slice_fusion.4
  17.2 0.5 slice_dynamic-update-slice_fusion.3
  17.7 0.5 constant_dynamic-update-slice_fusion
  18.2 0.8 slice_dynamic-update-slice_fusion.2
  19.0 0.5 slice_dynamic-update-slice_fusion.1
  19.5 0.5 fusion.8
  20.0 0.8 slice_dynamic-update-slice_fusion
  20.8 7.1 %fusion.35 = (f32[2,32]{1,0:T(2,128)S(1)}, f32[2,32]{1,0:T(2,128)S(1)}, f32[2,8,480,32,4]{2,3,4,1,0:T(8,128)}) fusion(bf16[32,4,1152,1,1]{2,1,0,4,3:T(4,128)(2,1)S(1)} %bitcast.100, bf16[2,8,480,1152]{3,2,1,0:T(8,128)(2,1)S(1)} %slice_dynamic-update-slice_fusion), kind=kOutput, calls=%fused_computation.54 | convolution fusion | flops 2267873280 | bytes 21922304 | tf_op jit(solution)/shard_map/dot_general | solution.py:46
  27.9 3.9 %all-reduce.4 = (f32[2,32]{1,0:T(2,128)S(1)}, f32[2,32]{1,0:T(2,128)S(1)}) all-reduce(f32[2,32]{1,0:T(2,128)S(1)} %get-tuple-element.6, f32[2,32]{1,0:T(2,128)S(1)} %get-tuple-element.5), channel_id=1, replica_groups=mesh['tm'=16,'rows'=2] {'rows'}, use_global_device_ids=true, to_apply=%region_3.4 | all-reduce | flops 128 | bytes 1024 | tf_op jit(solution)/shard_map/psum | solution.py:53
  31.8 2.9 %subtract_multiply_fusion = f32[2,8,480,32,4]{2,3,4,1,0:T(8,128)S(1)} fusion(f32[2,8,480,32,4]{2,3,4,1,0:T(8,128)} %get-tuple-element.13, f32[2,32]{1,0:T(2,128)S(1)} %get-tuple-element.12, f32[2,32]{1,0:T(2,128)S(1)} %get-tuple-element.11), kind=kLoop, calls=%fused_computation.7 | loop fusion | flops 1966080 | bytes 7864832 | tf_op jit(solution)/shard_map/mul | solution.py:57
  34.7 0.0 copy-start.2
  34.7 0.0 copy-start.3
  34.7 2.4 %copy.16 = f32[2,8,480,32,4]{2,1,4,3,0:T(8,128)S(1)} copy(f32[2,8,480,32,4]{2,3,4,1,0:T(8,128)S(1)} %subtract_multiply_fusion) | data formatting | bytes 7864320 | tf_op jit(solution)/shard_map/mul | solution.py:57
  37.2 0.0 copy-done.2
  37.2 0.0 copy-done.3
  37.2 1.4 multiply_convert_fusion
  38.7 3.4 %copy.17 = bf16[2,8,480,128]{3,1,0,2:T(8,128)(2,1)} copy(bf16[2,8,480,128]{2,1,3,0:T(8,128)(2,1)S(1)} %multiply_convert_fusion) | data formatting | bytes 3932160 | tf_op jit(solution)/shard_map/convert_element_type | solution.py:61
  42.0 0.0 copy-start.1
  42.0 54.3 %all_to_all.36 = bf16[2,8,480,128]{3,1,0,2:T(8,128)(2,1)S(1)} all-to-all(bf16[2,8,480,128]{3,1,0,2:T(8,128)(2,1)} %copy.17), channel_id=1, replica_groups=mesh['tm'=16,'rows'=2] {'tm'}, dimensions={2} | all-to-all | bytes 3932160 | tf_op jit(solution)/shard_map/all_to_all | solution.py:62
  96.4 0.3 copy.19
  96.7 0.0 copy-done.1
  96.7 0.7 fusion.22
  97.4 0.7 fusion.24
  98.0 0.9 add_convert_fusion.2
  99.0 0.6 fusion.17
  99.6 0.7 fusion.19
  100.3 1.0 add_convert_fusion.1
  101.3 0.7 fusion.12
  102.0 0.7 fusion.14
  102.6 1.0 add_convert_fusion
  103.6 49.4 %all_to_all.37 = bf16[32,8,30,128]{3,1,2,0:T(8,128)(2,1)S(1)} all-to-all(bf16[32,8,30,128]{3,1,2,0:T(8,128)(2,1)S(1)} %add_convert_fusion), channel_id=1, replica_groups=mesh['tm'=16,'rows'=2] {'tm'}, dimensions={0} | all-to-all | bytes 3932160 | tf_op jit(solution)/shard_map/all_to_all | solution.py:67
  153.0 0.1 copy.20
  153.1 1.5 copy.21
  (1 shorter events, 0.0 us)
Async XLA Ops:
  1.1 8.6 %collective-permute-start = (bf16[2,1,480,128]{3,2,1,0:T(8,128)(2,1)S(1)}, bf16[2,1,480,128]{3,2,1,0:T(8,128)(2,1)S(1)}, u32[]{:S(2)}, u32[]{:S(2)}) collective-permute-start(bf16[2,1,480,128]{3,2,1,0:T(8,128)(2,1)S(1)} %get-tuple-element.9), channel_id=1, source_target_pairs={{0,1},{2,3},{4,5},{6,7},{8,9},{10,11},{12,13},{14,15},{16,17},{18,... | collective-permute-start | bytes 737288 | tf_op jit(solution)/shard_map/ppermute | solution.py:16
  5.1 8.4 %collective-permute-start.1 = (bf16[2,1,480,128]{3,2,1,0:T(8,128)(2,1)S(1)}, bf16[2,1,480,128]{3,2,1,0:T(8,128)(2,1)S(1)}, u32[]{:S(2)}, u32[]{:S(2)}) collective-permute-start(bf16[2,1,480,128]{3,2,1,0:T(8,128)(2,1)S(1)} %get-tuple-element.10), channel_id=1, source_target_pairs={{1,0},{3,2},{5,4},{7,6},{9,8},{11,10},{13,12},{15,14},{17,16},{19,... | collective-permute-start | bytes 737288 | tf_op jit(solution)/shard_map/ppermute | solution.py:17
  7.6 8.3 %copy-start = (bf16[2,8,480,128]{3,2,1,0:T(8,128)(2,1)S(1)}, bf16[2,8,480,128]{3,2,1,0:T(8,128)(2,1)}, u32[]{:S(2)}) copy-start(bf16[2,8,480,128]{3,2,1,0:T(8,128)(2,1)} %param.5) | copy-start | bytes 5898244
  34.7 2.5 %copy-start.2 = (f32[128]{0:T(128)S(1)}, f32[128]{0:T(128)}, u32[]{:S(2)}) copy-start(f32[128]{0:T(128)} %param.8) | copy-start | bytes 1540
  34.7 2.5 %copy-start.3 = (f32[128]{0:T(128)S(1)}, f32[128]{0:T(128)}, u32[]{:S(2)}) copy-start(f32[128]{0:T(128)} %param.7) | copy-start | bytes 1540
  42.0 54.7 %copy-start.1 = (bf16[3,3,128,128]{3,2,1,0:T(8,128)(2,1)S(1)}, bf16[3,3,128,128]{3,2,1,0:T(8,128)(2,1)}, u32[]{:S(2)}) copy-start(bf16[3,3,128,128]{3,2,1,0:T(8,128)(2,1)} %param.9) | copy-start | bytes 884740
where the time goes:
time: 155 us
  blocking collectives  108 us (70%)
  local copies, waits for them, and re-layouts  14.3 us (9%)
  matrix products  13.9 us (9%)
  other arithmetic  7.38 us (5%)
  waiting for transfers between devices  5.84 us (4%)
  starting transfers between devices  5.28 us (3%)
    all_to_all x1, blocking collectives, body(): lax.all_to_all(hidden, 'tm', split_axis=2, concat_axis=0, tiled=True)  54.3 us
    all_to_all x1, blocking collectives, body(): lax.all_to_all(current, 'tm', split_axis=0, concat_axis=2, tiled=True)  49.4 us
    dot_general x1, matrix products, body(): jnp.dot(patches, spatial_weight.reshape(9 * chans, chans), preferred_elem...  7.06 us
    dot_general x9, matrix products, temporal_layer(): jnp.einsum('trwc,cd->trwd', extended[start:start + own], kernels[tap_inde...  6.82 us
    ppermute x1, starting transfers between devices, padded_2(): before = lax.ppermute(last, axis, up)  3.99 us
    psum x1, blocking collectives, body(): total_sum, total_square = lax.psum((part_sum, part_square), 'rows')  3.95 us
    ppermute x1, waiting for transfers between devices, padded_2(): after = lax.ppermute(leading, axis, down)  3.81 us
    unnamed x14, local copies, waits for them, and re-layouts  3.41 us
  transfers between devices with their start and end apart: 2, of which 2 were waited for; matrix products, arithmetic and copies ran while one was open for 1% of the time, Pallas kernels for 0%

commit v1 on v0

--- a/solution.py
+++ b/solution.py
@@ -4,6 +4,28 @@
 from jax.sharding import PartitionSpec as P
 
 GROUPS = 32
+
+
+def split_up(x, dim, size):
+    before, after = (x.shape[:dim], x.shape[dim + 1 :])
+    return jnp.moveaxis(x.reshape(*before, size, -1, *after), dim, 0)
+
+
+def joined_along(parts, dim):
+    parts = jnp.moveaxis(parts, 0, dim)
+    dims = parts.shape
+    return parts.reshape(*dims[:dim], dims[dim] * dims[dim + 1], *dims[dim + 2 :])
+
+
+def exchange_in_pairs(x, axis, split_dim, concat_dim):
+    size, index = (lax.axis_size(axis), lax.axis_index(axis))
+    blocks = split_up(x, split_dim, size)
+    finished = [blocks[index]]
+    for step in range(1, size):
+        sent = blocks[index ^ step]
+        finished.append(lax.ppermute(sent, axis, [(i, i ^ step) for i in range(size)]))
+    blocks = jnp.stack(finished)[index ^ jnp.arange(size)]
+    return joined_along(blocks, concat_dim)
 
 
 def padded_2(array, sides, width):
@@ -59,7 +81,7 @@
     ]
     normed = normed.reshape(fr_local, band, width, chans) * norm_gain + norm_shift
     hidden = jax.nn.silu(normed).astype(jnp.bfloat16)
-    current = lax.all_to_all(hidden, "tm", split_axis=2, concat_axis=0, tiled=True)
+    current = exchange_in_pairs(hidden, "tm", 2, 0)
     for layer, dilation in enumerate((1, 2, 4)):
         lead = 2 * dilation
         extended = jnp.pad(current, ((lead, 0), (0, 0), (0, 0), (0, 0)))

time: 155 us -> 234 us (1.51)
  local copies, waits for them, and re-layouts: 14.3 us -> 95.9 us
  blocking collectives: 108 us -> 60.7 us
  starting transfers between devices: 5.28 us -> 37.9 us
  other arithmetic: 7.38 us -> 13.4 us
  waiting for transfers between devices: 5.84 us -> 10.6 us
    all_to_all x1 -> x0, blocking collectives: 54.3 us -> none  [body(): lax.all_to_all(hidden, 'tm', split_axis=2, concat_axis=0, tiled=True)]
    another operation x0 -> x18, local copies, waits for them, and re-layouts: none -> 52.2 us
    ppermute x0 -> x15, starting transfers between devices: none -> 32.6 us  [exchange_in_pairs(): lax.ppermute(sent, axis, [(i, i ^ step) for i in range(size)])]
    unnamed x14 -> x41, local copies, waits for them, and re-layouts: 3.41 us -> 17.8 us
    reshape x0 -> x1, local copies, waits for them, and re-layouts: none -> 14.1 us  [body(): normed.reshape(fr_local, band, width, chans) * norm_gain + norm_shift]
    all_to_all x1, blocking collectives: 49.4 us -> 57 us  [body(): lax.all_to_all(current, 'tm', split_axis=0, concat_axis=2, tiled=True)]
    convert_element_type x1, other arithmetic: 1.45 us -> 8.68 us  [body(): hidden = jax.nn.silu(normed).astype(jnp.bfloat16)]
    ppermute x0 -> x15, waiting for transfers between devices: none -> 4.97 us  [exchange_in_pairs(): lax.ppermute(sent, axis, [(i, i ^ step) for i in range(size)])]
  transfers between devices with their start and end apart: 2 -> 17, of which waited for: 2 -> 4; matrix products, arithmetic and copies ran while one was open for 1% -> 18% of each run, Pallas kernels for 0% -> 0%
where the time goes in v1:
time: 234 us; the launch traced here: 233 us
  local copies, waits for them, and re-layouts  95.9 us (41%)
  blocking collectives  60.7 us (26%)
  starting transfers between devices  37.9 us (16%)
  matrix products  14 us (6%)
  other arithmetic  13.4 us (6%)
  waiting for transfers between devices  10.6 us (5%)
    all_to_all x1, blocking collectives, body(): lax.all_to_all(current, 'tm', split_axis=0, concat_axis=2, tiled=True)  57 us
    another operation x17, local copies, waits for them, and re-layouts  51.6 us
    ppermute x15, starting transfers between devices, exchange_in_pairs(): lax.ppermute(sent, axis, [(i, i ^ step) for i in range(size)])  32.6 us
    unnamed x41, local copies, waits for them, and re-layouts  17.8 us
    reshape x1, local copies, waits for them, and re-layouts, body(): normed.reshape(fr_local, band, width, chans) * norm_gain + norm_shift  14.1 us
    convert_element_type x1, other arithmetic, body(): hidden = jax.nn.silu(normed).astype(jnp.bfloat16)  8.68 us
    dot_general x1, matrix products, body(): jnp.dot(patches, spatial_weight.reshape(9 * chans, chans), preferred_elem...  7.05 us
    dot_general x9, matrix products, temporal_layer(): jnp.einsum('trwc,cd->trwd', extended[start:start + own], kernels[tap_inde...  6.94 us
  transfers between devices with their start and end apart: 17, of which 4 were waited for; matrix products, arithmetic and copies ran while one was open for 18% of the time, Pallas kernels for 0%

profile of v1, /device:TPU:1, one launch (start us, length us, event | category | flops | bytes accessed | tf_op | source)
XLA Modules:
  0.0 233.0 jit_solution(14676388461508914094)
XLA Ops:
  0.0 1.2 fusion.37
  1.2 4.0 %collective-permute-start = (bf16[2,1,480,128]{3,2,1,0:T(8,128)(2,1)S(1)}, bf16[2,1,480,128]{3,2,1,0:T(8,128)(2,1)S(1)}, u32[]{:S(2)}, u32[]{:S(2)}) collective-permute-start(bf16[2,1,480,128]{3,2,1,0:T(8,128)(2,1)S(1)} %get-tuple-element.25), channel_id=1, source_target_pairs={{0,1},{2,3},{4,5},{6,7},{8,9},{10,11},{12,13},{14,15},{16,17},{18,... | collective-permute-start | bytes 737288 | tf_op jit(solution)/shard_map/ppermute | solution.py:38
  5.2 1.3 collective-permute-start.1
  6.6 1.2 copy.7
  8.0 1.9 collective-permute-done
  9.8 3.8 %collective-permute-done.1 = bf16[2,1,480,128]{3,2,1,0:T(8,128)(2,1)S(1)} collective-permute-done((bf16[2,1,480,128]{3,2,1,0:T(8,128)(2,1)S(1)}, bf16[2,1,480,128]{3,2,1,0:T(8,128)(2,1)S(1)}, u32[]{:S(2)}, u32[]{:S(2)}) %collective-permute-start.1) | collective-permute-done | bytes 245792 | tf_op jit(solution)/shard_map/ppermute | solution.py:39
  13.6 0.9 fusion.7
  15.3 0.8 slice_dynamic-update-slice_fusion.4
  17.1 0.8 slice_dynamic-update-slice_fusion.2
  18.9 0.8 slice_dynamic-update-slice_fusion
  19.7 7.1 %fusion.36 = (f32[2,32]{1,0:T(2,128)S(1)}, f32[2,32]{1,0:T(2,128)S(1)}, f32[2,8,480,32,4]{2,3,4,1,0:T(8,128)}) fusion(bf16[32,4,1152,1,1]{2,1,0,4,3:T(4,128)(2,1)S(1)} %bitcast.147, bf16[2,8,480,1152]{3,2,1,0:T(8,128)(2,1)S(1)} %slice_dynamic-update-slice_fusion), kind=kOutput, calls=%fused_computation.90 | convolution fusion | flops 2267873280 | bytes 21922304 | tf_op jit(solution)/shard_map/dot_general | solution.py:68
  26.8 3.8 %all-reduce.4 = (f32[2,32]{1,0:T(2,128)S(1)}, f32[2,32]{1,0:T(2,128)S(1)}) all-reduce(f32[2,32]{1,0:T(2,128)S(1)} %get-tuple-element.6, f32[2,32]{1,0:T(2,128)S(1)} %get-tuple-element.5), channel_id=1, replica_groups=mesh['tm'=16,'rows'=2] {'rows'}, use_global_device_ids=true, to_apply=%region_3.4 | all-reduce | flops 128 | bytes 1024 | tf_op jit(solution)/shard_map/psum | solution.py:75
  30.5 2.9 %subtract_multiply_fusion = f32[2,8,480,32,4]{2,3,4,1,0:T(8,128)S(1)} fusion(f32[2,8,480,32,4]{2,3,4,1,0:T(8,128)} %get-tuple-element.29, f32[2,32]{1,0:T(2,128)S(1)} %get-tuple-element.28, f32[2,32]{1,0:T(2,128)S(1)} %get-tuple-element.27), kind=kLoop, calls=%fused_computation.8 | loop fusion | flops 1966080 | bytes 7864832 | tf_op jit(solution)/shard_map/mul | solution.py:79
  33.4 4.4 %copy.9 = f32[2,8,480,32,4]{2,1,4,3,0:T(8,128)} copy(f32[2,8,480,32,4]{2,3,4,1,0:T(8,128)S(1)} %subtract_multiply_fusion) | data formatting | bytes 7864320 | tf_op jit(solution)/shard_map/mul | solution.py:79
  37.8 14.1 %reshape.86 = f32[2,8,16,30,128]{3,2,1,4,0:T(8,128)} reshape(f32[2,8,480,32,4]{2,1,4,3,0:T(8,128)} %copy.9) | data formatting | bytes 7864320 | tf_op jit(solution)/shard_map/reshape | solution.py:82
  51.9 8.7 %multiply_convert_fusion = bf16[2,8,16,30,128]{3,2,1,4,0:T(8,128)(2,1)S(1)} fusion(f32[2,8,16,30,128]{3,2,1,4,0:T(8,128)} %reshape.86, f32[128]{0:T(128)S(1)} %copy-done.8, f32[128]{0:T(128)S(1)} %copy-done.9), kind=kLoop, calls=%fused_computation.3 | loop fusion | flops 6881280 | bytes 5899264 | tf_op jit(solution)/shard_map/convert_element_type | solution.py:83
  60.6 21.4 %constant_dynamic-slice_fusion = (bf16[2,8,1,30,128]{3,2,1,4,0:T(2,128)(2,1)S(1)}, bf16[2,8,1,30,128]{3,2,1,4,0:T(2,128)(2,1)S(1)}, bf16[2,8,1,30,128]{3,2,1,4,0...) fusion(bf16[2,8,16,30,128]{3,2,1,4,0:T(8,128)(2,1)S(1)} %multip, ...), kind=kLoop, calls=%fused_computation.70 | loop fusion | bytes 3932224 | tf_op jit(solution)/shard_map/dynamic-slice.15
  82.0 1.6 copy.10
  83.6 2.2 copy.11
  85.9 3.0 %collective-permute-start.2 = (bf16[2,8,30,128]{3,1,2,0:T(8,128)(2,1)}, bf16[2,8,30,128]{3,1,2,0:T(8,128)(2,1)}, u32[]{:S(2)}, u32[]{:S(2)}) collective-permute-start(bf16[2,8,30,128]{3,1,2,0:T(8,128)(2,1)} %bitcast.6), channel_id=1, source_target_pairs={{0,2},{2,0},{4,6},{6,4},{8,10},{10,8},{12,14},{14,12},{16,18},{18,... | collective-permute-start | bytes 368648 | tf_op jit(solution)/shard_map/ppermute | solution.py:26
  88.9 2.2 copy.12
  91.1 1.2 collective-permute-start.3
  92.3 2.2 copy.13
  95.0 2.2 copy.14
  97.2 1.3 collective-permute-start.5
  98.5 2.2 copy.15
  101.3 2.2 copy.16
  103.6 2.2 copy.17
  105.8 2.2 copy.18
  108.0 2.2 copy.19
  110.3 2.2 copy.20
  112.5 2.2 copy.21
  114.7 1.6 copy.22
  116.4 0.7 copy.23
  117.1 0.9 copy.24
  118.1 0.7 copy.25
  118.8 0.7 bitcast_dynamic-update-slice_fusion.15
  119.4 2.2 collective-permute-start.7
  121.7 1.6 bitcast_dynamic-update-slice_fusion.14
  123.5 1.6 bitcast_dynamic-update-slice_fusion.13
  125.1 2.3 collective-permute-start.9
  127.4 1.6 bitcast_dynamic-update-slice_fusion.12
  129.4 1.6 bitcast_dynamic-update-slice_fusion.11
  131.0 3.3 %collective-permute-start.11 = (bf16[2,8,30,128]{3,1,2,0:T(8,128)(2,1)S(1)}, bf16[2,8,30,128]{3,1,2,0:T(8,128)(2,1)S(1)}, u32[]{:S(2)}, u32[]{:S(2)}) collective-permute-start(bf16[2,8,30,128]{3,1,2,0:T(8,128)(2,1)S(1)} %bitcast.153), channel_id=1, source_target_pairs={{0,20},{2,22},{4,16},{6,18},{8,28},{10,30},{12,24},{14,26},{16,4},... | collective-permute-start | bytes 368648 | tf_op jit(solution)/shard_map/ppermute | solution.py:26
  134.2 1.6 bitcast_dynamic-update-slice_fusion.10
  136.7 3.3 %collective-permute-start.13 = (bf16[2,8,30,128]{3,1,2,0:T(8,128)(2,1)S(1)}, bf16[2,8,30,128]{3,1,2,0:T(8,128)(2,1)S(1)}, u32[]{:S(2)}, u32[]{:S(2)}) collective-permute-start(bf16[2,8,30,128]{3,1,2,0:T(8,128)(2,1)S(1)} %bitcast.151), channel_id=1, source_target_pairs={{0,24},{2,26},{4,28},{6,30},{8,16},{10,18},{12,20},{14,22},{16,8},... | collective-permute-start | bytes 368648 | tf_op jit(solution)/shard_map/ppermute | solution.py:26
  140.6 7.4 %collective-permute-start.14 = (bf16[2,8,30,128]{3,1,2,0:T(8,128)(2,1)S(1)}, bf16[2,8,30,128]{3,1,2,0:T(8,128)(2,1)S(1)}, u32[]{:S(2)}, u32[]{:S(2)}) collective-permute-start(bf16[2,8,30,128]{3,1,2,0:T(8,128)(2,1)S(1)} %bitcast.150), channel_id=1, source_target_pairs={{0,26},{2,24},{4,30},{6,28},{8,18},{10,16},{12,22},{14,20},{16,10}... | collective-permute-start | bytes 368648 | tf_op jit(solution)/shard_map/ppermute | solution.py:26
  148.7 2.6 %collective-permute-start.15 = (bf16[2,8,30,128]{3,1,2,0:T(8,128)(2,1)S(1)}, bf16[2,8,30,128]{3,1,2,0:T(8,128)(2,1)S(1)}, u32[]{:S(2)}, u32[]{:S(2)}) collective-permute-start(bf16[2,8,30,128]{3,1,2,0:T(8,128)(2,1)S(1)} %bitcast.149), channel_id=1, source_target_pairs={{0,28},{2,30},{4,24},{6,26},{8,20},{10,22},{12,16},{14,18},{16,12}... | collective-permute-start | bytes 368648 | tf_op jit(solution)/shard_map/ppermute | solution.py:26
  152.0 0.9 collective-permute-done.11
  152.9 4.0 %collective-permute-start.16 = (bf16[2,8,30,128]{3,1,2,0:T(8,128)(2,1)S(1)}, bf16[2,8,30,128]{3,1,2,0:T(8,128)(2,1)S(1)}, u32[]{:S(2)}, u32[]{:S(2)}) collective-permute-start(bf16[2,8,30,128]{3,1,2,0:T(8,128)(2,1)S(1)} %bitcast.148), channel_id=1, source_target_pairs={{0,30},{2,28},{4,26},{6,24},{8,22},{10,20},{12,18},{14,16},{16,14}... | collective-permute-start | bytes 368648 | tf_op jit(solution)/shard_map/ppermute | solution.py:26
  157.5 4.0 %collective-permute-done.12 = bf16[2,8,30,128]{3,1,2,0:T(8,128)(2,1)S(1)} collective-permute-done((bf16[2,8,30,128]{3,1,2,0:T(8,128)(2,1)S(1)}, bf16[2,8,30,128]{3,1,2,0:T(8,128)(2,1)S(1)}, u32[]{:S(2)}, u32[]{:S(2)}) %collective-permute-start.12) | collective-permute-done | bytes 122912 | tf_op jit(solution)/shard_map/ppermute | solution.py:26
  162.2 0.7 bitcast_dynamic-update-slice_fusion.3
  162.9 0.7 bitcast_dynamic-update-slice_fusion.2
  163.5 0.7 bitcast_dynamic-update-slice_fusion.1
  164.2 0.7 bitcast_dynamic-update-slice_fusion
  164.9 2.5 %gather_fusion = bf16[16,2,8,30,128]{4,2,3,1,0:T(8,128)(2,1)S(1)} fusion(bf16[16,2,8,30,128]{4,2,3,1,0:T(8,128)(2,1)} %bitcast_dynamic-update-slice_fusion, s32[1024]{0:T(1024)S(1)} %pad_clamp_fusion), kind=kCustom, calls=%fused_computation | custom fusion | bytes 3932224 | tf_op jit(solution)/shard_map/gather | solution.py:27
  167.4 0.7 fusion.22
  168.7 1.1 add_convert_fusion.2
  170.4 0.7 fusion.19
  171.1 1.0 add_convert_fusion.1
  172.7 0.7 fusion.14
  173.4 1.0 add_convert_fusion
  174.3 57.0 %all_to_all.18 = bf16[32,8,30,128]{3,1,2,0:T(8,128)(2,1)S(1)} all-to-all(bf16[32,8,30,128]{3,1,2,0:T(8,128)(2,1)S(1)} %add_convert_fusion), channel_id=1, replica_groups=mesh['tm'=16,'rows'=2] {'tm'}, dimensions={0} | all-to-all | bytes 3932160 | tf_op jit(solution)/shard_map/all_to_all | solution.py:89
  231.4 1.5 copy.27
  (58 shorter events, 10.9 us)
Async XLA Ops:
  0.0 13.6 %copy-start = (bf16[2,8,480,128]{3,2,1,0:T(8,128)(2,1)S(1)}, bf16[2,8,480,128]{3,2,1,0:T(8,128)(2,1)}, u32[]{:S(2)}) copy-start(bf16[2,8,480,128]{3,2,1,0:T(8,128)(2,1)} %param.5) | copy-start | bytes 5898244
  1.2 8.6 %collective-permute-start = (bf16[2,1,480,128]{3,2,1,0:T(8,128)(2,1)S(1)}, bf16[2,1,480,128]{3,2,1,0:T(8,128)(2,1)S(1)}, u32[]{:S(2)}, u32[]{:S(2)}) collective-permute-start(bf16[2,1,480,128]{3,2,1,0:T(8,128)(2,1)S(1)} %get-tuple-element.25), channel_id=1, source_target_pairs={{0,1},{2,3},{4,5},{6,7},{8,9},{10,11},{12,13},{14,15},{16,17},{18,... | collective-permute-start | bytes 737288 | tf_op jit(solution)/shard_map/ppermute | solution.py:38
  5.2 8.4 %collective-permute-start.1 = (bf16[2,1,480,128]{3,2,1,0:T(8,128)(2,1)S(1)}, bf16[2,1,480,128]{3,2,1,0:T(8,128)(2,1)S(1)}, u32[]{:S(2)}, u32[]{:S(2)}) collective-permute-start(bf16[2,1,480,128]{3,2,1,0:T(8,128)(2,1)S(1)} %get-tuple-element.26), channel_id=1, source_target_pairs={{1,0},{3,2},{5,4},{7,6},{9,8},{11,10},{13,12},{15,14},{17,16},{19,... | collective-permute-start | bytes 737288 | tf_op jit(solution)/shard_map/ppermute | solution.py:39
  37.8 14.1 %copy-start.8 = (f32[128]{0:T(128)S(1)}, f32[128]{0:T(128)}, u32[]{:S(2)}) copy-start(f32[128]{0:T(128)} %param.8) | copy-start | bytes 1540
  37.8 14.1 %copy-start.9 = (f32[128]{0:T(128)S(1)}, f32[128]{0:T(128)}, u32[]{:S(2)}) copy-start(f32[128]{0:T(128)} %param.7) | copy-start | bytes 1540
  85.9 33.5 %collective-permute-start.2 = (bf16[2,8,30,128]{3,1,2,0:T(8,128)(2,1)}, bf16[2,8,30,128]{3,1,2,0:T(8,128)(2,1)}, u32[]{:S(2)}, u32[]{:S(2)}) collective-permute-start(bf16[2,8,30,128]{3,1,2,0:T(8,128)(2,1)} %bitcast.6), channel_id=1, source_target_pairs={{0,2},{2,0},{4,6},{6,4},{8,10},{10,8},{12,14},{14,12},{16,18},{18,... | collective-permute-start | bytes 368648 | tf_op jit(solution)/shard_map/ppermute | solution.py:26
  91.1 32.1 %collective-permute-start.3 = (bf16[2,8,30,128]{3,1,2,0:T(8,128)(2,1)}, bf16[2,8,30,128]{3,1,2,0:T(8,128)(2,1)}, u32[]{:S(2)}, u32[]{:S(2)}) collective-permute-start(bf16[2,8,30,128]{3,1,2,0:T(8,128)(2,1)} %bitcast.8), channel_id=1, source_target_pairs={{0,4},{2,6},{4,0},{6,2},{8,12},{10,14},{12,8},{14,10},{16,20},{18,... | collective-permute-start | bytes 368648 | tf_op jit(solution)/shard_map/ppermute | solution.py:26
  94.6 30.5 %collective-permute-start.4 = (bf16[2,8,30,128]{3,1,2,0:T(8,128)(2,1)}, bf16[2,8,30,128]{3,1,2,0:T(8,128)(2,1)}, u32[]{:S(2)}, u32[]{:S(2)}) collective-permute-start(bf16[2,8,30,128]{3,1,2,0:T(8,128)(2,1)} %bitcast.10), channel_id=1, source_target_pairs={{0,6},{2,4},{4,2},{6,0},{8,14},{10,12},{12,10},{14,8},{16,22},{18,... | collective-permute-start | bytes 368648 | tf_op jit(solution)/shard_map/ppermute | solution.py:26
  97.2 31.7 %collective-permute-start.5 = (bf16[2,8,30,128]{3,1,2,0:T(8,128)(2,1)}, bf16[2,8,30,128]{3,1,2,0:T(8,128)(2,1)}, u32[]{:S(2)}, u32[]{:S(2)}) collective-permute-start(bf16[2,8,30,128]{3,1,2,0:T(8,128)(2,1)} %bitcast.12), channel_id=1, source_target_pairs={{0,8},{2,10},{4,12},{6,14},{8,0},{10,2},{12,4},{14,6},{16,24},{18,... | collective-permute-start | bytes 368648 | tf_op jit(solution)/shard_map/ppermute | solution.py:26
  100.8 30.2 %collective-permute-start.6 = (bf16[2,8,30,128]{3,1,2,0:T(8,128)(2,1)}, bf16[2,8,30,128]{3,1,2,0:T(8,128)(2,1)}, u32[]{:S(2)}, u32[]{:S(2)}) collective-permute-start(bf16[2,8,30,128]{3,1,2,0:T(8,128)(2,1)} %bitcast.14), channel_id=1, source_target_pairs={{0,10},{2,8},{4,14},{6,12},{8,2},{10,0},{12,6},{14,4},{16,26},{18,... | collective-permute-start | bytes 368648 | tf_op jit(solution)/shard_map/ppermute | solution.py:26
  117.1 2.3 %copy-start.7 = (bf16[2,8,1,30,128]{4,1,3,0,2:T(8,128)(2,1)S(1)}, bf16[2,8,1,30,128]{4,1,3,0,2:T(8,128)(2,1)}, u32[]{:S(2)}) copy-start(bf16[2,8,1,30,128]{4,1,3,0,2:T(8,128)(2,1)} %copy.16) | copy-start | bytes 368644
  117.1 6.1 %copy-start.6 = (bf16[2,8,1,30,128]{4,1,3,0,2:T(8,128)(2,1)S(1)}, bf16[2,8,1,30,128]{4,1,3,0,2:T(8,128)(2,1)}, u32[]{:S(2)}) copy-start(bf16[2,8,1,30,128]{4,1,3,0,2:T(8,128)(2,1)} %copy.17) | copy-start | bytes 368644
  117.1 8.0 %copy-start.5 = (bf16[2,8,1,30,128]{4,1,3,0,2:T(8,128)(2,1)S(1)}, bf16[2,8,1,30,128]{4,1,3,0,2:T(8,128)(2,1)}, u32[]{:S(2)}) copy-start(bf16[2,8,1,30,128]{4,1,3,0,2:T(8,128)(2,1)} %copy.18) | copy-start | bytes 368644
  117.1 11.9 %copy-start.4 = (bf16[2,8,1,30,128]{4,1,3,0,2:T(8,128)(2,1)S(1)}, bf16[2,8,1,30,128]{4,1,3,0,2:T(8,128)(2,1)}, u32[]{:S(2)}) copy-start(bf16[2,8,1,30,128]{4,1,3,0,2:T(8,128)(2,1)} %copy.19) | copy-start | bytes 368644
  117.1 13.9 %copy-start.3 = (bf16[2,8,1,30,128]{4,1,3,0,2:T(8,128)(2,1)S(1)}, bf16[2,8,1,30,128]{4,1,3,0,2:T(8,128)(2,1)}, u32[]{:S(2)}) copy-start(bf16[2,8,1,30,128]{4,1,3,0,2:T(8,128)(2,1)} %copy.20) | copy-start | bytes 368644
  117.1 18.7 %copy-start.2 = (bf16[2,8,1,30,128]{4,1,3,0,2:T(8,128)(2,1)S(1)}, bf16[2,8,1,30,128]{4,1,3,0,2:T(8,128)(2,1)}, u32[]{:S(2)}) copy-start(bf16[2,8,1,30,128]{4,1,3,0,2:T(8,128)(2,1)} %copy.21) | copy-start | bytes 368644
  119.4 16.4 %collective-permute-start.7 = (bf16[2,8,30,128]{3,1,2,0:T(8,128)(2,1)S(1)}, bf16[2,8,30,128]{3,1,2,0:T(8,128)(2,1)S(1)}, u32[]{:S(2)}, u32[]{:S(2)}) collective-permute-start(bf16[2,8,30,128]{3,1,2,0:T(8,128)(2,1)S(1)} %bitcast.157), channel_id=1, source_target_pairs={{0,12},{2,14},{4,8},{6,10},{8,4},{10,6},{12,0},{14,2},{16,28},{18,... | collective-permute-start | bytes 368648 | tf_op jit(solution)/shard_map/ppermute | solution.py:26
  123.2 13.5 %collective-permute-start.8 = (bf16[2,8,30,128]{3,1,2,0:T(8,128)(2,1)S(1)}, bf16[2,8,30,128]{3,1,2,0:T(8,128)(2,1)S(1)}, u32[]{:S(2)}, u32[]{:S(2)}) collective-permute-start(bf16[2,8,30,128]{3,1,2,0:T(8,128)(2,1)S(1)} %bitcast.156), channel_id=1, source_target_pairs={{0,14},{2,12},{4,10},{6,8},{8,6},{10,4},{12,2},{14,0},{16,30},{18,... | collective-permute-start | bytes 368648 | tf_op jit(solution)/shard_map/ppermute | solution.py:26
  125.1 15.5 %collective-permute-start.9 = (bf16[2,8,30,128]{3,1,2,0:T(8,128)(2,1)S(1)}, bf16[2,8,30,128]{3,1,2,0:T(8,128)(2,1)S(1)}, u32[]{:S(2)}, u32[]{:S(2)}) collective-permute-start(bf16[2,8,30,128]{3,1,2,0:T(8,128)(2,1)S(1)} %bitcast.155), channel_id=1, source_target_pairs={{0,16},{2,18},{4,20},{6,22},{8,24},{10,26},{12,28},{14,30},{16,0},... | collective-permute-start | bytes 368648 | tf_op jit(solution)/shard_map/ppermute | solution.py:26
  129.0 19.7 %collective-permute-start.10 = (bf16[2,8,30,128]{3,1,2,0:T(8,128)(2,1)S(1)}, bf16[2,8,30,128]{3,1,2,0:T(8,128)(2,1)S(1)}, u32[]{:S(2)}, u32[]{:S(2)}) collective-permute-start(bf16[2,8,30,128]{3,1,2,0:T(8,128)(2,1)S(1)} %bitcast.154), channel_id=1, source_target_pairs={{0,18},{2,16},{4,22},{6,20},{8,26},{10,24},{12,30},{14,28},{16,2},... | collective-permute-start | bytes 368648 | tf_op jit(solution)/shard_map/ppermute | solution.py:26
  131.0 21.9 %collective-permute-start.11 = (bf16[2,8,30,128]{3,1,2,0:T(8,128)(2,1)S(1)}, bf16[2,8,30,128]{3,1,2,0:T(8,128)(2,1)S(1)}, u32[]{:S(2)}, u32[]{:S(2)}) collective-permute-start(bf16[2,8,30,128]{3,1,2,0:T(8,128)(2,1)S(1)} %bitcast.153), channel_id=1, source_target_pairs={{0,20},{2,22},{4,16},{6,18},{8,28},{10,30},{12,24},{14,26},{16,4},... | collective-permute-start | bytes 368648 | tf_op jit(solution)/shard_map/ppermute | solution.py:26
  135.8 25.8 %collective-permute-start.12 = (bf16[2,8,30,128]{3,1,2,0:T(8,128)(2,1)S(1)}, bf16[2,8,30,128]{3,1,2,0:T(8,128)(2,1)S(1)}, u32[]{:S(2)}, u32[]{:S(2)}) collective-permute-start(bf16[2,8,30,128]{3,1,2,0:T(8,128)(2,1)S(1)} %bitcast.152), channel_id=1, source_target_pairs={{0,22},{2,20},{4,18},{6,16},{8,30},{10,28},{12,26},{14,24},{16,6},... | collective-permute-start | bytes 368648 | tf_op jit(solution)/shard_map/ppermute | solution.py:26
  136.7 25.5 %collective-permute-start.13 = (bf16[2,8,30,128]{3,1,2,0:T(8,128)(2,1)S(1)}, bf16[2,8,30,128]{3,1,2,0:T(8,128)(2,1)S(1)}, u32[]{:S(2)}, u32[]{:S(2)}) collective-permute-start(bf16[2,8,30,128]{3,1,2,0:T(8,128)(2,1)S(1)} %bitcast.151), channel_id=1, source_target_pairs={{0,24},{2,26},{4,28},{6,30},{8,16},{10,18},{12,20},{14,22},{16,8},... | collective-permute-start | bytes 368648 | tf_op jit(solution)/shard_map/ppermute | solution.py:26
  140.6 22.2 %collective-permute-start.14 = (bf16[2,8,30,128]{3,1,2,0:T(8,128)(2,1)S(1)}, bf16[2,8,30,128]{3,1,2,0:T(8,128)(2,1)S(1)}, u32[]{:S(2)}, u32[]{:S(2)}) collective-permute-start(bf16[2,8,30,128]{3,1,2,0:T(8,128)(2,1)S(1)} %bitcast.150), channel_id=1, source_target_pairs={{0,26},{2,24},{4,30},{6,28},{8,18},{10,16},{12,22},{14,20},{16,10}... | collective-permute-start | bytes 368648 | tf_op jit(solution)/shard_map/ppermute | solution.py:26
  148.7 14.8 %collective-permute-start.15 = (bf16[2,8,30,128]{3,1,2,0:T(8,128)(2,1)S(1)}, bf16[2,8,30,128]{3,1,2,0:T(8,128)(2,1)S(1)}, u32[]{:S(2)}, u32[]{:S(2)}) collective-permute-start(bf16[2,8,30,128]{3,1,2,0:T(8,128)(2,1)S(1)} %bitcast.149), channel_id=1, source_target_pairs={{0,28},{2,30},{4,24},{6,26},{8,20},{10,22},{12,16},{14,18},{16,12}... | collective-permute-start | bytes 368648 | tf_op jit(solution)/shard_map/ppermute | solution.py:26
  152.9 11.3 %collective-permute-start.16 = (bf16[2,8,30,128]{3,1,2,0:T(8,128)(2,1)S(1)}, bf16[2,8,30,128]{3,1,2,0:T(8,128)(2,1)S(1)}, u32[]{:S(2)}, u32[]{:S(2)}) collective-permute-start(bf16[2,8,30,128]{3,1,2,0:T(8,128)(2,1)S(1)} %bitcast.148), channel_id=1, source_target_pairs={{0,30},{2,28},{4,26},{6,24},{8,22},{10,20},{12,18},{14,16},{16,14}... | collective-permute-start | bytes 368648 | tf_op jit(solution)/shard_map/ppermute | solution.py:26
  162.9 4.5 %copy-start.1 = (bf16[3,3,128,128]{3,2,1,0:T(8,128)(2,1)S(1)}, bf16[3,3,128,128]{3,2,1,0:T(8,128)(2,1)}, u32[]{:S(2)}) copy-start(bf16[3,3,128,128]{3,2,1,0:T(8,128)(2,1)} %param.9) | copy-start | bytes 884740
